TPU v7x, 32 devices: a whole 2x2x4 slice. The times are simulated.
32 devices in a mesh: groups: 2 (over y), tm: 4 (over z), space: 2 (over x), clip: 2 (over core).
Axes of the slice: x: 2, y: 2, z: 4, core: 2. Of those that a mesh axis runs over, the one named last changes fastest.
Arguments:
- features: bfloat16 [4, 16, 8, 16, 256], P(('groups', 'clip'), 'tm', 'space'), parts along dimension 0, may hold values from -6 to 6
- frame_counts: int32 [4], P(('groups', 'clip')), parts along dimension 0, may hold values from 1 to 16, as said below
- routes: int32 [4, 512, 1], P(('groups', 'clip'), ('tm', 'space')), parts along dimension 0, may hold values from 0 to 7; in each aligned block of 64 rows (0 to 63, 64 to 127, ..., all dimensions but the last counted through in order) at most 9 rows name the same one
- norm_gains: float32 [3, 256], replicated, may hold values from 0.5 to 1.5
- conv_weights: bfloat16 [2, 256, 27, 256], P(None, 'tm'), may hold values from -0.078125 to 0.078125
- conv_biases: float32 [2, 256], replicated, may hold values from -3 to 3
- latent_weight: bfloat16 [256, 16], replicated, may hold values from -0.375 to 0.375
- embed_weight: bfloat16 [64, 3072], replicated, may hold values from -0.75 to 0.75
- embed_bias: float32 [3072], replicated, may hold values from -3 to 3
Outputs:
- packed: bfloat16 [4, 576, 3072], P(('groups', 'clip'), ('tm', 'space')), parts along dimension 0
There are 2 independent parts, one for each index of `groups`. A program takes and returns all parts, laid end to end along the dimension named above; an argument that names none is the same for every part. Nothing has to cross between parts.
Inputs may be any that keep to these rules, and one draw needn't show every extreme that they name: `routes`: in each clip, the 64 patches of one span and tile name any one owner at most 9 times. `frame_counts`: one clip of each part has all 16 frames valid.
All inputs are finite; a program needn't handle non-finite values.
Results may differ from a plain program's by a relative error of at most 0.0054.
Values may be sent and summed in bfloat16 or wider, within the bound.
A program may use at most 64 MiB of HBM per device.

v0:
```python
import jax
import jax.numpy as jnp
from jax import lax
from jax.sharding import PartitionSpec as P


def shifted(block, axis, distance):
    devices = range(lax.axis_size(axis))
    route = [(i - distance, i) for i in devices if i - distance in devices]
    return lax.ppermute(block, axis, route)


def with_halo(cells, sides, width):
    for axis, dim in sides:
        count = lax.axis_size(axis)
        ends = count - 1
        head = lax.slice_in_dim(cells, 0, width, axis=dim)
        tail = lax.slice_in_dim(cells, cells.shape[dim] - width, cells.shape[dim], axis=dim)
        cells = jnp.concatenate(
            [
                lax.ppermute(tail, axis, [(i, (i + 1) % count) for i in range(ends)]),
                cells,
                lax.ppermute(head, axis, [((i + 1) % count, i) for i in range(ends)]),
            ],
            axis=dim,
        )
    return cells


def norm_silu(values, gain):
    scale = lax.rsqrt(jnp.mean(values * values, axis=-1, keepdims=True) + 1e-06)
    return jax.nn.silu(values * scale * gain)


def conv_taps(padded, weights):
    frames = padded.shape[0] - 2
    rows = padded.shape[1] - 2
    cols = padded.shape[2] - 2
    inner = padded.shape[3]
    outer = weights.shape[0]
    summed = jnp.zeros((frames * rows * cols, outer), jnp.float32)
    for frame_tap in range(3):
        columns = jnp.concatenate(
            [
                padded[
                    frame_tap : frame_tap + frames,
                    row_tap : row_tap + rows,
                    col_tap : col_tap + cols,
                ]
                for row_tap in range(3)
                for col_tap in range(3)
            ],
            axis=-1,
        )
        columns = columns.reshape(frames * rows * cols, 9 * inner)
        taps = weights[:, 9 * frame_tap : 9 * frame_tap + 9, :].reshape(outer, 9 * inner)
        summed = summed + lax.dot_general(
            columns, taps, (((1,), (1,)), ((), ())), preferred_element_type=jnp.float32
        )
    return summed.reshape(frames, rows, cols, outer)


def causal_layer(active, weights):
    earlier = shifted(active[-2:], "tm", 1)
    extended = jnp.concatenate([earlier, active], axis=0)
    rimmed = with_halo(extended, (("space", 1),), 1)
    padded = jnp.pad(rimmed, ((0, 0), (0, 0), (1, 1), (0, 0)))
    copies = lax.axis_size(("space", "clip"))
    share = weights.shape[2] // copies
    mine = lax.dynamic_slice_in_dim(weights, lax.axis_index(("space", "clip")) * share, share, 2)
    slices = lax.all_gather(mine, "tm", axis=0, tiled=True)
    return conv_taps(padded, lax.all_gather(slices, ("space", "clip"), axis=2, tiled=True))


def shards(
    features,
    frame_counts,
    routes,
    norm_gains,
    conv_weights,
    conv_biases,
    latent_weight,
    embed_weight,
    embed_bias,
):
    inputs = features[0].astype(jnp.float32)
    frames, rows, cols, width = inputs.shape
    active = norm_silu(inputs, norm_gains[0]).astype(jnp.bfloat16)
    hidden = causal_layer(active, conv_weights[0]) + conv_biases[0]
    active = norm_silu(hidden, norm_gains[1]).astype(jnp.bfloat16)
    hidden = causal_layer(active, conv_weights[1]) + conv_biases[1]
    merged = inputs + hidden
    active = norm_silu(merged, norm_gains[2]).astype(jnp.bfloat16)
    latent = jnp.dot(active.reshape(-1, width), latent_weight, preferred_element_type=jnp.float32)
    channels = latent_weight.shape[1]
    latent = latent.reshape(frames, rows // 2, 2, cols // 2, 2, channels)
    patches = latent.transpose(0, 1, 3, 2, 4, 5).reshape(-1, 4 * channels).astype(jnp.bfloat16)
    tok_count = patches.shape[0]
    owners = lax.axis_size("tm") * lax.axis_size("space")
    most_rows = (tok_count + owners - 1) // owners + 1
    destinations = routes[0, :, 0]
    positions = jnp.arange(tok_count, dtype=jnp.int32)
    before = positions[:, None] > positions[None, :]
    ranks = jnp.sum(
        ((destinations[:, None] == destinations[None, :]) & before).astype(jnp.int32), axis=1
    )
    targets = destinations * most_rows + ranks
    frame_ids = lax.axis_index("tm") * frames + positions // (rows // 2 * (cols // 2))
    alive = (frame_ids < frame_counts[0]).astype(jnp.bfloat16)
    placing = (jnp.arange(owners * most_rows, dtype=jnp.int32)[:, None] == targets[None, :]).astype(
        jnp.bfloat16
    )
    outgoing = jnp.dot(placing, patches, preferred_element_type=jnp.float32).astype(jnp.bfloat16)
    outgoing = outgoing.reshape(owners, most_rows, 4 * channels)
    marks = jnp.dot(placing, alive[:, None], preferred_element_type=jnp.float32).astype(
        jnp.bfloat16
    )
    marks = marks.reshape(owners, most_rows)
    tokens = lax.all_to_all(outgoing, ("tm", "space"), split_axis=0, concat_axis=0, tiled=True)
    flags = lax.all_to_all(marks, ("tm", "space"), split_axis=0, concat_axis=0, tiled=True)
    projected = (
        jnp.dot(
            tokens.reshape(-1, tokens.shape[2]), embed_weight, preferred_element_type=jnp.float32
        )
        + embed_bias
    )
    projected = projected * flags.reshape(-1, 1).astype(jnp.float32)
    packed_rows = projected.astype(jnp.bfloat16).reshape(tokens.shape[0], tokens.shape[1], -1)
    return packed_rows.reshape(1, -1, packed_rows.shape[2])


def solution(mesh):
    return jax.shard_map(
        shards,
        mesh=mesh,
        in_specs=(
            P(("groups", "clip"), "tm", "space", None, None),
            P(("groups", "clip")),
            P(("groups", "clip"), ("tm", "space"), None),
            P(),
            P(None, "tm", None, None),
            P(),
            P(),
            P(),
            P(),
        ),
        out_specs=P(("groups", "clip"), ("tm", "space"), None),
        check_vma=False,
    )
```

profile of v0, /device:TPU:0, one launch (start us, length us, event | category | flops | bytes accessed | tf_op | source)
XLA Modules:
  0.0 164.7 jit_solution(14299890801617923095)
XLA Ops:
  6.5 1.6 fusion.52
  8.6 39.7 %all-gather = bf16[1,256,27,64]{3,2,0,1:T(8,128)(2,1)S(1)} all-gather(bf16[1,64,27,64]{3,2,0,1:T(8,128)(2,1)S(1)} %copy.34), channel_id=2, replica_groups=mesh['groups'=2,'tm'=4,'space'=2,'clip'=2] {'tm'}, dimensions={1}, use_global_device_ids=true | all-gather | bytes 1105920 | tf_op jit(solution)/shard_map/all_gather | solution.py:71
  48.3 2.7 %copy.25 = bf16[1,256,27,64]{1,3,2,0:T(8,128)(2,1)} copy(bf16[1,256,27,64]{3,2,0,1:T(8,128)(2,1)S(1)} %all-gather) | data formatting | bytes 1769472 | tf_op jit(solution)/shard_map/all_gather | solution.py:71
  51.6 37.3 %all-gather.2 = bf16[1,256,27,64]{3,2,0,1:T(8,128)(2,1)S(1)} all-gather(bf16[1,64,27,64]{3,2,0,1:T(8,128)(2,1)S(1)} %copy.36), channel_id=4, replica_groups=mesh['groups'=2,'tm'=4,'space'=2,'clip'=2] {'tm'}, dimensions={1}, use_global_device_ids=true | all-gather | bytes 1105920 | tf_op jit(solution)/shard_map/all_gather | solution.py:71
  88.9 2.7 %copy.27 = bf16[1,256,27,64]{1,3,2,0:T(8,128)(2,1)} copy(bf16[1,256,27,64]{3,2,0,1:T(8,128)(2,1)S(1)} %all-gather.2) | data formatting | bytes 1769472 | tf_op jit(solution)/shard_map/all_gather | solution.py:71
  92.0 3.5 %collective-permute-start = (bf16[2,4,16,256]{3,2,1,0:T(8,128)(2,1)S(1)}, bf16[2,4,16,256]{3,2,1,0:T(8,128)(2,1)S(1)}, u32[]{:S(2)}, u32[]{:S(2)}) collective-permute-start(bf16[2,4,16,256]{3,2,1,0:T(8,128)(2,1)S(1)} %slice.322), channel_id=1, source_target_pairs={{0,4},{4,8},{8,12},{1,5},{5,9},{9,13},{2,6},{6,10},{10,14},{3,7},{... | collective-permute-start | bytes 196616 | tf_op jit(solution)/shard_map/ppermute | solution.py:10
  95.7 1.7 %collective-permute-done = bf16[2,4,16,256]{3,2,1,0:T(8,128)(2,1)S(1)} collective-permute-done((bf16[2,4,16,256]{3,2,1,0:T(8,128)(2,1)S(1)}, bf16[2,4,16,256]{3,2,1,0:T(8,128)(2,1)S(1)}, u32[]{:S(2)}, u32[]{:S(2)}) %collective-permute-start) | collective-permute-done | bytes 65568 | tf_op jit(solution)/shard_map/ppermute | solution.py:10
  97.4 3.4 %collective-permute-start.1 = (bf16[6,1,16,256]{3,2,1,0:T(8,128)(2,1)S(1)}, bf16[6,1,16,256]{3,2,1,0:T(8,128)(2,1)S(1)}, u32[]{:S(2)}, u32[]{:S(2)}) collective-permute-start(bf16[6,1,16,256]{3,2,1,0:T(8,128)(2,1)S(1)} %get-tuple-element.71), channel_id=1, source_target_pairs={{0,2},{1,3},{4,6},{5,7},{8,10},{9,11},{12,14},{13,15},{16,18},{17,... | collective-permute-start | bytes 147464 | tf_op jit(solution)/shard_map/ppermute | solution.py:21
  100.8 1.3 collective-permute-start.2
  103.3 4.6 %collective-permute-done.2 = bf16[6,1,16,256]{3,2,1,0:T(8,128)(2,1)S(1)} collective-permute-done((bf16[6,1,16,256]{3,2,1,0:T(8,128)(2,1)S(1)}, bf16[6,1,16,256]{3,2,1,0:T(8,128)(2,1)S(1)}, u32[]{:S(2)}, u32[]{:S(2)}) %collective-permute-start.2) | collective-permute-done | bytes 49184 | tf_op jit(solution)/shard_map/ppermute | solution.py:23
  108.3 0.8 slice_dynamic-update-slice_fusion.31
  109.1 0.8 slice_dynamic-update-slice_fusion.30
  109.8 0.8 slice_dynamic-update-slice_fusion.29
  110.6 0.8 slice_dynamic-update-slice_fusion.28
  111.4 0.8 fusion.27
  112.2 0.8 slice_dynamic-update-slice_fusion.27
  113.1 0.8 slice_dynamic-update-slice_fusion.26
  113.8 0.8 slice_dynamic-update-slice_fusion.25
  114.6 0.8 slice_dynamic-update-slice_fusion.24
  115.4 2.2 %fusion.51 = (bf16[256,9,256]{0,2,1:T(8,128)(2,1)S(1)}, bf16[256,9,256]{0,2,1:T(8,128)(2,1)S(1)}, bf16[256,9,256]{0,2,1:T(8,128)(2,1)S(1)}) fusion(bf16[256,27,256]{0,2,1:T(8,128)(2,1)} %bitcast.85), kind=kLoop, calls=%fused_computation.153 | loop fusion | bytes 7077888 | tf_op jit(solution)/shard_map/slice | solution.py:56
  117.6 1.7 %fusion.56 = f32[256,256]{1,0:T(8,128)S(1)} fusion(bf16[256,2304]{1,0:T(8,128)(2,1)} %bitcast.4, bf16[256,2304]{0,1:T(8,128)(2,1)S(1)} %bitcast.83), kind=kOutput, calls=%fused_computation.158 | convolution fusion | flops 301989888 | bytes 2621440 | tf_op jit(solution)/shard_map/dot_general | solution.py:57
  119.4 1.8 %convolution_add_fusion.4 = f32[256,256]{1,0:T(8,128)S(1)} fusion(f32[256,256]{1,0:T(8,128)S(1)} %fusion.56, bf16[256,2304]{1,0:T(8,128)(2,1)} %bitcast.7, bf16[256,2304]{0,1:T(8,128)(2,1)S(1)} %bitcast.82), kind=kOutput, calls=%fused_computation.9 | convolution fusion | flops 302055424 | bytes 2883584 | tf_op jit(solution)/shard_map/dot_general | solution.py:57
  122.0 4.3 %collective-permute-start.3 = (bf16[2,4,16,256]{3,2,1,0:T(8,128)(2,1)S(1)}, bf16[2,4,16,256]{3,2,1,0:T(8,128)(2,1)S(1)}, u32[]{:S(2)}, u32[]{:S(2)}) collective-permute-start(bf16[2,4,16,256]{3,2,1,0:T(8,128)(2,1)S(1)} %slice.356), channel_id=1, source_target_pairs={{0,4},{4,8},{8,12},{1,5},{5,9},{9,13},{2,6},{6,10},{10,14},{3,7},{... | collective-permute-start | bytes 196616 | tf_op jit(solution)/shard_map/ppermute | solution.py:10
  127.1 4.4 %all-to-all-start.1 = ((bf16[8,1,9]{2,1,0:T(2,128)(2,1)}), bf16[8,1,9]{2,1,0:T(2,128)(2,1)S(1)}, u32[]{:S(2)}, u32[]{:S(2)}) async-start(bf16[8,1,9]{2,1,0:T(2,128)(2,1)} %all_to_all.12), calls=%async_computation.1 | async-start | bytes 8192 | tf_op jit(solution)/shard_map/all_to_all | solution.py:120
  131.5 3.9 %collective-permute-start.4 = (bf16[6,1,16,256]{3,2,1,0:T(8,128)(2,1)S(1)}, bf16[6,1,16,256]{3,2,1,0:T(8,128)(2,1)S(1)}, u32[]{:S(2)}, u32[]{:S(2)}) collective-permute-start(bf16[6,1,16,256]{3,2,1,0:T(8,128)(2,1)S(1)} %get-tuple-element.65), channel_id=1, source_target_pairs={{0,2},{1,3},{4,6},{5,7},{8,10},{9,11},{12,14},{13,15},{16,18},{17,... | collective-permute-start | bytes 147464 | tf_op jit(solution)/shard_map/ppermute | solution.py:21
  135.4 1.3 collective-permute-start.5
  136.7 2.2 %fusion.50 = (bf16[256,9,256]{0,2,1:T(8,128)(2,1)S(1)}, bf16[256,9,256]{0,2,1:T(8,128)(2,1)S(1)}, bf16[256,9,256]{0,2,1:T(8,128)(2,1)S(1)}) fusion(bf16[256,27,256]{0,2,1:T(8,128)(2,1)} %bitcast.84), kind=kLoop, calls=%fused_computation.152 | loop fusion | bytes 7077888 | tf_op jit(solution)/shard_map/slice | solution.py:56
  139.0 2.4 %collective-permute-done.5 = bf16[6,1,16,256]{3,2,1,0:T(8,128)(2,1)S(1)} collective-permute-done((bf16[6,1,16,256]{3,2,1,0:T(8,128)(2,1)S(1)}, bf16[6,1,16,256]{3,2,1,0:T(8,128)(2,1)S(1)}, u32[]{:S(2)}, u32[]{:S(2)}) %collective-permute-start.5) | collective-permute-done | bytes 49184 | tf_op jit(solution)/shard_map/ppermute | solution.py:23
  144.9 0.7 reshape.170
  145.6 4.5 %all-to-all-start = ((bf16[8,2,288]{2,1,0:T(2,128)(2,1)}), bf16[8,2,288]{2,1,0:T(2,128)(2,1)S(1)}, u32[]{:S(2)}, u32[]{:S(2)}) async-start(bf16[8,2,288]{2,1,0:T(2,128)(2,1)} %reshape.170), calls=%async_computation | async-start | bytes 24576 | tf_op jit(solution)/shard_map/all_to_all | solution.py:119
  150.3 6.4 %all-to-all-done = bf16[8,2,288]{2,1,0:T(2,128)(2,1)S(1)} async-done(((bf16[8,2,288]{2,1,0:T(2,128)(2,1)}), bf16[8,2,288]{2,1,0:T(2,128)(2,1)S(1)}, u32[]{:S(2)}, u32[]{:S(2)}) %all-to-all-start) | async-done | bytes 9248 | tf_op jit(solution)/shard_map/all_to_all | solution.py:119
  156.9 1.0 fusion.2
  (76 shorter events, 7.7 us)
Async XLA Ops:
  6.5 150.3 %copy-start = (bf16[64,3072]{1,0:T(8,128)(2,1)S(1)}, bf16[64,3072]{1,0:T(8,128)(2,1)}, u32[]{:S(2)}) copy-start(bf16[64,3072]{1,0:T(8,128)(2,1)} %param.16) | copy-start | bytes 1179652
  6.5 108.9 %all-gather.7.cloned.1.call-start = ((), (), s32[]{:S(2)}) async-start(), calls=%async_computation.2 | async-start | bytes 4423680 | tf_op jit(solution)/shard_map/all_gather | solution.py:72
  51.1 85.7 %all-gather.9.cloned.1.call-start = ((), (), s32[]{:S(2)}) async-start(), calls=%async_computation.3 | async-start | bytes 4423680 | tf_op jit(solution)/shard_map/all_gather | solution.py:72
  88.9 2.7 %copy-start.1 = (bf16[1,4,4,16,256]{4,3,2,1,0:T(8,128)(2,1)S(1)}, bf16[1,4,4,16,256]{4,3,2,1,0:T(8,128)(2,1)}, u32[]{:S(2)}) copy-start(bf16[1,4,4,16,256]{4,3,2,1,0:T(8,128)(2,1)} %param.9) | copy-start | bytes 393220
  88.9 2.9 %copy-start.4 = (f32[3,256]{1,0:T(4,128)S(1)}, f32[3,256]{1,0:T(4,128)}, u32[]{:S(2)}) copy-start(f32[3,256]{1,0:T(4,128)} %param.12) | copy-start | bytes 9220
  91.6 3.9 %copy-start.5 = (f32[2,256]{1,0:T(2,128)S(1)}, f32[2,256]{1,0:T(2,128)}, u32[]{:S(2)}) copy-start(f32[2,256]{1,0:T(2,128)} %param.14) | copy-start | bytes 6148
  91.6 3.9 %copy-start.6 = (s32[1,64,1]{1,2,0:T(1,128)S(1)}, s32[1,64,1]{1,2,0:T(1,128)}, u32[]{:S(2)}) copy-start(s32[1,64,1]{1,2,0:T(1,128)} %param.11) | copy-start | bytes 772
  92.0 5.4 %collective-permute-start = (bf16[2,4,16,256]{3,2,1,0:T(8,128)(2,1)S(1)}, bf16[2,4,16,256]{3,2,1,0:T(8,128)(2,1)S(1)}, u32[]{:S(2)}, u32[]{:S(2)}) collective-permute-start(bf16[2,4,16,256]{3,2,1,0:T(8,128)(2,1)S(1)} %slice.322), channel_id=1, source_target_pairs={{0,4},{4,8},{8,12},{1,5},{5,9},{9,13},{2,6},{6,10},{10,14},{3,7},{... | collective-permute-start | bytes 196616 | tf_op jit(solution)/shard_map/ppermute | solution.py:10
  97.4 5.9 %collective-permute-start.1 = (bf16[6,1,16,256]{3,2,1,0:T(8,128)(2,1)S(1)}, bf16[6,1,16,256]{3,2,1,0:T(8,128)(2,1)S(1)}, u32[]{:S(2)}, u32[]{:S(2)}) collective-permute-start(bf16[6,1,16,256]{3,2,1,0:T(8,128)(2,1)S(1)} %get-tuple-element.71), channel_id=1, source_target_pairs={{0,2},{1,3},{4,6},{5,7},{8,10},{9,11},{12,14},{13,15},{16,18},{17,... | collective-permute-start | bytes 147464 | tf_op jit(solution)/shard_map/ppermute | solution.py:21
  100.8 7.2 %collective-permute-start.2 = (bf16[6,1,16,256]{3,2,1,0:T(8,128)(2,1)S(1)}, bf16[6,1,16,256]{3,2,1,0:T(8,128)(2,1)S(1)}, u32[]{:S(2)}, u32[]{:S(2)}) collective-permute-start(bf16[6,1,16,256]{3,2,1,0:T(8,128)(2,1)S(1)} %get-tuple-element.72), channel_id=1, source_target_pairs={{2,0},{3,1},{6,4},{7,5},{10,8},{11,9},{14,12},{15,13},{18,16},{19,... | collective-permute-start | bytes 147464 | tf_op jit(solution)/shard_map/ppermute | solution.py:23
  122.0 9.5 %collective-permute-start.3 = (bf16[2,4,16,256]{3,2,1,0:T(8,128)(2,1)S(1)}, bf16[2,4,16,256]{3,2,1,0:T(8,128)(2,1)S(1)}, u32[]{:S(2)}, u32[]{:S(2)}) collective-permute-start(bf16[2,4,16,256]{3,2,1,0:T(8,128)(2,1)S(1)} %slice.356), channel_id=1, source_target_pairs={{0,4},{4,8},{8,12},{1,5},{5,9},{9,13},{2,6},{6,10},{10,14},{3,7},{... | collective-permute-start | bytes 196616 | tf_op jit(solution)/shard_map/ppermute | solution.py:10
  127.1 18.6 %all-to-all-start.1 = ((bf16[8,1,9]{2,1,0:T(2,128)(2,1)}), bf16[8,1,9]{2,1,0:T(2,128)(2,1)S(1)}, u32[]{:S(2)}, u32[]{:S(2)}) async-start(bf16[8,1,9]{2,1,0:T(2,128)(2,1)} %all_to_all.12), calls=%async_computation.1 | async-start | bytes 8192 | tf_op jit(solution)/shard_map/all_to_all | solution.py:120
  131.5 7.5 %collective-permute-start.4 = (bf16[6,1,16,256]{3,2,1,0:T(8,128)(2,1)S(1)}, bf16[6,1,16,256]{3,2,1,0:T(8,128)(2,1)S(1)}, u32[]{:S(2)}, u32[]{:S(2)}) collective-permute-start(bf16[6,1,16,256]{3,2,1,0:T(8,128)(2,1)S(1)} %get-tuple-element.65), channel_id=1, source_target_pairs={{0,2},{1,3},{4,6},{5,7},{8,10},{9,11},{12,14},{13,15},{16,18},{17,... | collective-permute-start | bytes 147464 | tf_op jit(solution)/shard_map/ppermute | solution.py:21
  135.4 6.0 %collective-permute-start.5 = (bf16[6,1,16,256]{3,2,1,0:T(8,128)(2,1)S(1)}, bf16[6,1,16,256]{3,2,1,0:T(8,128)(2,1)S(1)}, u32[]{:S(2)}, u32[]{:S(2)}) collective-permute-start(bf16[6,1,16,256]{3,2,1,0:T(8,128)(2,1)S(1)} %get-tuple-element.66), channel_id=1, source_target_pairs={{2,0},{3,1},{6,4},{7,5},{10,8},{11,9},{14,12},{15,13},{18,16},{19,... | collective-permute-start | bytes 147464 | tf_op jit(solution)/shard_map/ppermute | solution.py:23
  143.6 0.7 copy-start.3
  143.6 13.3 %copy-start.2 = (f32[3072]{0:T(1024)S(1)}, f32[3072]{0:T(1024)}, u32[]{:S(2)}) copy-start(f32[3072]{0:T(1024)} %param.17) | copy-start | bytes 36868
  145.6 11.1 %all-to-all-start = ((bf16[8,2,288]{2,1,0:T(2,128)(2,1)}), bf16[8,2,288]{2,1,0:T(2,128)(2,1)S(1)}, u32[]{:S(2)}, u32[]{:S(2)}) async-start(bf16[8,2,288]{2,1,0:T(2,128)(2,1)} %reshape.170), calls=%async_computation | async-start | bytes 24576 | tf_op jit(solution)/shard_map/all_to_all | solution.py:119
Sparse Core Ops, SparseCore 0:
  51.2 32.3 all-gather.6
  91.8 33.0 all-gather.8
where the time goes:
time: 165 us
  blocking collectives  77 us (47%)
  starting transfers between devices  26.6 us (16%)
  local copies, waits for them, and re-layouts  21.5 us (13%)
  waiting for transfers between devices  15.8 us (10%)
  between operations  14.5 us (9%)
  matrix products  7 us (4%)
  other arithmetic  2.28 us (1%)
    all_gather x2, blocking collectives, causal_layer(): slices = lax.all_gather(mine, 'tm', axis=0, tiled=True)  77 us
    ppermute x2, starting transfers between devices, shifted(): return lax.ppermute(block, axis, route)  7.8 us
    unnamed x32, local copies, waits for them, and re-layouts  7.52 us
    ppermute x2, starting transfers between devices, with_halo(): lax.ppermute(tail, axis, [(i, (i + 1) % count) for i in range(ends)])  7.32 us
    ppermute x2, waiting for transfers between devices, with_halo(): lax.ppermute(head, axis, [((i + 1) % count, i) for i in range(ends)])  7.07 us
    all_to_all x1, waiting for transfers between devices, shards(): lax.all_to_all(outgoing, ('tm', 'space'), split_axis=0, concat_axis=0, ti...  6.45 us
    dot_general x6, matrix products, conv_taps(): lax.dot_general(columns, taps, (((1,), (1,)), ((), ())), preferred_elemen...  5.49 us
    all_gather x2, local copies, waits for them, and re-layouts, causal_layer(): slices = lax.all_gather(mine, 'tm', axis=0, tiled=True)  5.42 us
  transfers between devices with their start and end apart: 10, of which 5 were waited for; matrix products, arithmetic and copies ran while one was open for 15% of the time, Pallas kernels for 0%

commit v1 on v0

--- a/solution.py
+++ b/solution.py
@@ -68,7 +68,20 @@
     copies = lax.axis_size(("space", "clip"))
     share = weights.shape[2] // copies
     mine = lax.dynamic_slice_in_dim(weights, lax.axis_index(("space", "clip")) * share, share, 2)
-    slices = lax.all_gather(mine, "tm", axis=0, tiled=True)
+
+    def supply_all_lots_all_in(target, net_axis="tm"):
+        lanes = lax.psum(1, axis_name=net_axis)
+        val2 = sorted(((u, (u + 1) % lanes) for u in range(lanes)))
+        t_next = target
+        buffer = [t_next]
+        for src_i in range(1, lanes):
+            t_next = lax.ppermute(t_next, axis_name=net_axis, perm=val2)
+            buffer.insert(0, t_next)
+        right_arr = jnp.concatenate(buffer, 0)
+        carry_out = lax.axis_index(net_axis)
+        return jnp.roll(right_arr, (carry_out + 1) * target.shape[0], 0)
+
+    slices = supply_all_lots_all_in(mine)
     return conv_taps(padded, lax.all_gather(slices, ("space", "clip"), axis=2, tiled=True))
 
 

time: 165 us -> 160 us (0.970)
  blocking collectives: 77 us -> 0 us
  waiting for transfers between devices: 15.8 us -> 85.2 us
  other arithmetic: 2.28 us -> 12.7 us
  local copies, waits for them, and re-layouts: 21.5 us -> 15.4 us
    all_gather x2 -> x0, blocking collectives: 77 us -> none  [causal_layer(): slices = lax.all_gather(mine, 'tm', axis=0, tiled=True)]
    ppermute x0 -> x6, waiting for transfers between devices: none -> 69.5 us  [supply_all_lots_all_in(): t_next = lax.ppermute(t_next, axis_name=net_axis, perm=val2)]
    concatenate x0 -> x2, other arithmetic: none -> 10.5 us  [supply_all_lots_all_in(): return jnp.roll(right_arr, (carry_out + 1) * target.shape[0], 0)]
    all_gather x2 -> x0, local copies, waits for them, and re-layouts: 5.42 us -> none  [causal_layer(): slices = lax.all_gather(mine, 'tm', axis=0, tiled=True)]
    ppermute x0 -> x6, starting transfers between devices: none -> 3.17 us  [supply_all_lots_all_in(): t_next = lax.ppermute(t_next, axis_name=net_axis, perm=val2)]
    ppermute x2, starting transfers between devices: 7.8 us -> 5.6 us  [shifted(): return lax.ppermute(block, axis, route)]
    unnamed x32 -> x30, local copies, waits for them, and re-layouts: 7.52 us -> 6.38 us
  transfers between devices with their start and end apart: 10 -> 16, of which waited for: 5 -> 11; matrix products, arithmetic and copies ran while one was open for 15% -> 15% of each run, Pallas kernels for 0% -> 0%
where the time goes in v1:
time: 160 us; the launch traced here: 159 us
  waiting for transfers between devices  85.2 us (53%)
  starting transfers between devices  25.7 us (16%)
  local copies, waits for them, and re-layouts  15.4 us (10%)
  between operations  14.5 us (9%)
  other arithmetic  12.7 us (8%)
  matrix products  5.72 us (4%)
    ppermute x6, waiting for transfers between devices, supply_all_lots_all_in(): t_next = lax.ppermute(t_next, axis_name=net_axis, perm=val2)  69.5 us
    concatenate x2, other arithmetic, supply_all_lots_all_in(): return jnp.roll(right_arr, (carry_out + 1) * target.shape[0], 0)  10.5 us
    ppermute x2, waiting for transfers between devices, with_halo(): lax.ppermute(head, axis, [((i + 1) % count, i) for i in range(ends)])  6.92 us
    all_to_all x1, waiting for transfers between devices, shards(): lax.all_to_all(outgoing, ('tm', 'space'), split_axis=0, concat_axis=0, ti...  6.45 us
    unnamed x30, local copies, waits for them, and re-layouts  6.38 us
    ppermute x2, starting transfers between devices, with_halo(): lax.ppermute(tail, axis, [(i, (i + 1) % count) for i in range(ends)])  6.33 us
    ppermute x2, starting transfers between devices, shifted(): return lax.ppermute(block, axis, route)  5.6 us
    all_to_all x1, starting transfers between devices, shards(): lax.all_to_all(outgoing, ('tm', 'space'), split_axis=0, concat_axis=0, ti...  4.58 us
  transfers between devices with their start and end apart: 16, of which 11 were waited for; matrix products, arithmetic and copies ran while one was open for 15% of the time, Pallas kernels for 0%

profile of v1, /device:TPU:0, one launch (start us, length us, event | category | flops | bytes accessed | tf_op | source)
XLA Modules:
  0.0 159.2 jit_solution(4425635512948171180)
XLA Ops:
  6.5 1.6 %fusion.66 = (bf16[1,64,27,256]{3,1,2,0:T(8,128)(2,1)S(1)}, bf16[1,64,27,256]{3,1,2,0:T(8,128)(2,1)S(1)}) fusion(bf16[2,64,27,256]{3,1,2,0:T(8,128)(2,1)} %param.15), kind=kLoop, calls=%fused_computation.184 | loop fusion | bytes 3538944 | tf_op jit(solution)/shard_map/slice | solution.py:104
  8.7 3.1 %collective-permute-start.3 = (bf16[64,27,64]{0,2,1:T(8,128)(2,1)S(1)}, bf16[64,27,64]{0,2,1:T(8,128)(2,1)S(1)}, u32[]{:S(2)}, u32[]{:S(2)}) collective-permute-start(bf16[64,27,64]{0,2,1:T(8,128)(2,1)S(1)} %bitcast.85), channel_id=1, source_target_pairs={{0,4},{4,8},{8,12},{12,0},{1,5},{5,9},{9,13},{13,1},{2,6},{6,10},{... | collective-permute-start | bytes 663560 | tf_op jit(solution)/shard_map/ppermute | solution.py:78
  11.8 12.2 %collective-permute-done.3 = bf16[64,27,64]{0,2,1:T(8,128)(2,1)S(1)} collective-permute-done((bf16[64,27,64]{0,2,1:T(8,128)(2,1)S(1)}, bf16[64,27,64]{0,2,1:T(8,128)(2,1)S(1)}, u32[]{:S(2)}, u32[]{:S(2)}) %collective-permute-start.3) | collective-permute-done | bytes 221216 | tf_op jit(solution)/shard_map/ppermute | solution.py:78
  24.0 13.1 %collective-permute-done.4 = bf16[64,27,64]{0,2,1:T(8,128)(2,1)S(1)} collective-permute-done((bf16[64,27,64]{0,2,1:T(8,128)(2,1)S(1)}, bf16[64,27,64]{0,2,1:T(8,128)(2,1)S(1)}, u32[]{:S(2)}, u32[]{:S(2)}) %collective-permute-start.4) | collective-permute-done | bytes 221216 | tf_op jit(solution)/shard_map/ppermute | solution.py:78
  37.2 12.3 %collective-permute-done.5 = bf16[64,27,64]{0,2,1:T(8,128)(2,1)S(1)} collective-permute-done((bf16[64,27,64]{0,2,1:T(8,128)(2,1)S(1)}, bf16[64,27,64]{0,2,1:T(8,128)(2,1)S(1)}, u32[]{:S(2)}, u32[]{:S(2)}) %collective-permute-start.5) | collective-permute-done | bytes 221216 | tf_op jit(solution)/shard_map/ppermute | solution.py:78
  49.4 5.2 %fusion.15 = bf16[256,27,64]{0,2,1:T(8,128)(2,1)} fusion(s32[]{:T(128)S(6)} %select_n.26, bf16[64,27,64]{0,2,1:T(8,128)(2,1)S(1)} %collective-permute-done.5, bf16[64,27,64]{0,2,1:T(8,128)(2,1)S(1)} %collective-permute-done.4, bf16[64,27,64]{0,2,1:T(8,128)(2,1)S(1)} %collective-permute-done.3, bf16[64,27,64]{0,2,1:T(8,128)(2,1)S(1)} %bitcast.86), kind=kLoop, calls=%fused_computation.41 | loop fusion | flops 7077888 | bytes 1769476 | tf_op jit(solution)/shard_map/jit(_roll_dynamic)/concatenate | solution.py:82
  55.1 11.4 %collective-permute-done.9 = bf16[64,27,64]{0,2,1:T(8,128)(2,1)S(1)} collective-permute-done((bf16[64,27,64]{0,2,1:T(8,128)(2,1)S(1)}, bf16[64,27,64]{0,2,1:T(8,128)(2,1)S(1)}, u32[]{:S(2)}, u32[]{:S(2)}) %collective-permute-start.9) | collective-permute-done | bytes 221216 | tf_op jit(solution)/shard_map/ppermute | solution.py:78
  66.6 10.4 %collective-permute-done.10 = bf16[64,27,64]{0,2,1:T(8,128)(2,1)S(1)} collective-permute-done((bf16[64,27,64]{0,2,1:T(8,128)(2,1)S(1)}, bf16[64,27,64]{0,2,1:T(8,128)(2,1)S(1)}, u32[]{:S(2)}, u32[]{:S(2)}) %collective-permute-start.10) | collective-permute-done | bytes 221216 | tf_op jit(solution)/shard_map/ppermute | solution.py:78
  77.1 10.1 %collective-permute-done.11 = bf16[64,27,64]{0,2,1:T(8,128)(2,1)S(1)} collective-permute-done((bf16[64,27,64]{0,2,1:T(8,128)(2,1)S(1)}, bf16[64,27,64]{0,2,1:T(8,128)(2,1)S(1)}, u32[]{:S(2)}, u32[]{:S(2)}) %collective-permute-start.11) | collective-permute-done | bytes 221216 | tf_op jit(solution)/shard_map/ppermute | solution.py:78
  87.1 5.3 %fusion.8 = bf16[256,27,64]{0,2,1:T(8,128)(2,1)} fusion(s32[]{:T(128)S(6)} %select_n.26, bf16[64,27,64]{0,2,1:T(8,128)(2,1)S(1)} %collective-permute-done.11, bf16[64,27,64]{0,2,1:T(8,128)(2,1)S(1)} %collective-permute-done.10, bf16[64,27,64]{0,2,1:T(8,128)(2,1)S(1)} %collective-permute-done.9, bf16[64,27,64]{0,2,1:T(8,128)(2,1)S(1)} %bitcast.88), kind=kLoop, calls=%fused_computation.34 | loop fusion | flops 7077888 | bytes 1769476 | tf_op jit(solution)/shard_map/jit(_roll_dynamic)/concatenate | solution.py:82
  92.6 1.3 collective-permute-start
  94.1 1.7 %collective-permute-done = bf16[2,4,16,256]{3,2,1,0:T(8,128)(2,1)S(1)} collective-permute-done((bf16[2,4,16,256]{3,2,1,0:T(8,128)(2,1)S(1)}, bf16[2,4,16,256]{3,2,1,0:T(8,128)(2,1)S(1)}, u32[]{:S(2)}, u32[]{:S(2)}) %collective-permute-start) | collective-permute-done | bytes 65568 | tf_op jit(solution)/shard_map/ppermute | solution.py:10
  95.8 2.5 %collective-permute-start.1 = (bf16[6,1,16,256]{3,2,1,0:T(8,128)(2,1)S(1)}, bf16[6,1,16,256]{3,2,1,0:T(8,128)(2,1)S(1)}, u32[]{:S(2)}, u32[]{:S(2)}) collective-permute-start(bf16[6,1,16,256]{3,2,1,0:T(8,128)(2,1)S(1)} %get-tuple-element.72), channel_id=1, source_target_pairs={{0,2},{1,3},{4,6},{5,7},{8,10},{9,11},{12,14},{13,15},{16,18},{17,... | collective-permute-start | bytes 147464 | tf_op jit(solution)/shard_map/ppermute | solution.py:21
  98.4 1.5 collective-permute-start.2
  101.0 4.5 %collective-permute-done.2 = bf16[6,1,16,256]{3,2,1,0:T(8,128)(2,1)S(1)} collective-permute-done((bf16[6,1,16,256]{3,2,1,0:T(8,128)(2,1)S(1)}, bf16[6,1,16,256]{3,2,1,0:T(8,128)(2,1)S(1)}, u32[]{:S(2)}, u32[]{:S(2)}) %collective-permute-start.2) | collective-permute-done | bytes 49184 | tf_op jit(solution)/shard_map/ppermute | solution.py:23
  105.8 0.7 slice_dynamic-update-slice_fusion.31
  107.2 0.8 slice_dynamic-update-slice_fusion.29
  108.0 0.7 slice_dynamic-update-slice_fusion.28
  109.4 0.7 slice_dynamic-update-slice_fusion.27
  110.1 0.7 slice_dynamic-update-slice_fusion.26
  111.5 0.7 slice_dynamic-update-slice_fusion.24
  112.3 2.2 %fusion.65 = (bf16[256,9,256]{0,2,1:T(8,128)(2,1)S(1)}, bf16[256,9,256]{0,2,1:T(8,128)(2,1)S(1)}, bf16[256,9,256]{0,2,1:T(8,128)(2,1)S(1)}) fusion(bf16[256,27,256]{0,2,1:T(8,128)(2,1)} %all-gather.3.cloned.1.call-done), kind=kLoop, calls=%fused_computation.183 | loop fusion | bytes 7077888 | tf_op jit(solution)/shard_map/slice | solution.py:56
  114.5 1.7 %fusion.70 = f32[256,256]{1,0:T(8,128)S(1)} fusion(bf16[256,2304]{1,0:T(8,128)(2,1)} %bitcast.4, bf16[256,2304]{0,1:T(8,128)(2,1)S(1)} %bitcast.83), kind=kOutput, calls=%fused_computation.188 | convolution fusion | flops 301989888 | bytes 2621440 | tf_op jit(solution)/shard_map/dot_general | solution.py:57
  117.6 4.3 %collective-permute-start.6 = (bf16[2,4,16,256]{3,2,1,0:T(8,128)(2,1)S(1)}, bf16[2,4,16,256]{3,2,1,0:T(8,128)(2,1)S(1)}, u32[]{:S(2)}, u32[]{:S(2)}) collective-permute-start(bf16[2,4,16,256]{3,2,1,0:T(8,128)(2,1)S(1)} %slice.356), channel_id=1, source_target_pairs={{0,4},{4,8},{8,12},{1,5},{5,9},{9,13},{2,6},{6,10},{10,14},{3,7},{... | collective-permute-start | bytes 196616 | tf_op jit(solution)/shard_map/ppermute | solution.py:10
  122.7 3.2 %all-to-all-start.1 = ((bf16[8,1,9]{2,1,0:T(2,128)(2,1)}), bf16[8,1,9]{2,1,0:T(2,128)(2,1)S(1)}, u32[]{:S(2)}, u32[]{:S(2)}) async-start(bf16[8,1,9]{2,1,0:T(2,128)(2,1)} %all_to_all.12), calls=%async_computation.1 | async-start | bytes 8192 | tf_op jit(solution)/shard_map/all_to_all | solution.py:133
  126.0 3.8 %collective-permute-start.7 = (bf16[6,1,16,256]{3,2,1,0:T(8,128)(2,1)S(1)}, bf16[6,1,16,256]{3,2,1,0:T(8,128)(2,1)S(1)}, u32[]{:S(2)}, u32[]{:S(2)}) collective-permute-start(bf16[6,1,16,256]{3,2,1,0:T(8,128)(2,1)S(1)} %get-tuple-element.66), channel_id=1, source_target_pairs={{0,2},{1,3},{4,6},{5,7},{8,10},{9,11},{12,14},{13,15},{16,18},{17,... | collective-permute-start | bytes 147464 | tf_op jit(solution)/shard_map/ppermute | solution.py:21
  129.9 1.3 collective-permute-start.8
  131.2 2.2 %fusion.64 = (bf16[256,9,256]{0,2,1:T(8,128)(2,1)S(1)}, bf16[256,9,256]{0,2,1:T(8,128)(2,1)S(1)}, bf16[256,9,256]{0,2,1:T(8,128)(2,1)S(1)}) fusion(bf16[256,27,256]{0,2,1:T(8,128)(2,1)} %all-gather.5.cloned.1.call-done), kind=kLoop, calls=%fused_computation.182 | loop fusion | bytes 7077888 | tf_op jit(solution)/shard_map/slice | solution.py:56
  133.4 2.4 %collective-permute-done.8 = bf16[6,1,16,256]{3,2,1,0:T(8,128)(2,1)S(1)} collective-permute-done((bf16[6,1,16,256]{3,2,1,0:T(8,128)(2,1)S(1)}, bf16[6,1,16,256]{3,2,1,0:T(8,128)(2,1)S(1)}, u32[]{:S(2)}, u32[]{:S(2)}) %collective-permute-start.8) | collective-permute-done | bytes 49184 | tf_op jit(solution)/shard_map/ppermute | solution.py:23
  140.1 4.6 %all-to-all-start = ((bf16[8,2,288]{2,1,0:T(2,128)(2,1)}), bf16[8,2,288]{2,1,0:T(2,128)(2,1)S(1)}, u32[]{:S(2)}, u32[]{:S(2)}) async-start(bf16[8,2,288]{2,1,0:T(2,128)(2,1)} %reshape.166), calls=%async_computation | async-start | bytes 24576 | tf_op jit(solution)/shard_map/all_to_all | solution.py:132
  144.8 6.4 %all-to-all-done = bf16[8,2,288]{2,1,0:T(2,128)(2,1)S(1)} async-done(((bf16[8,2,288]{2,1,0:T(2,128)(2,1)}), bf16[8,2,288]{2,1,0:T(2,128)(2,1)S(1)}, u32[]{:S(2)}, u32[]{:S(2)}) %all-to-all-start) | async-done | bytes 9248 | tf_op jit(solution)/shard_map/all_to_all | solution.py:132
  151.4 1.0 fusion.2
  (85 shorter events, 10.8 us)
Async XLA Ops:
  6.5 144.8 %copy-start = (bf16[64,3072]{1,0:T(8,128)(2,1)S(1)}, bf16[64,3072]{1,0:T(8,128)(2,1)}, u32[]{:S(2)}) copy-start(bf16[64,3072]{1,0:T(8,128)(2,1)} %param.18) | copy-start | bytes 1179652
  6.5 105.7 %all-gather.3.cloned.1.call-start = ((), (), s32[]{:S(2)}) async-start(), calls=%async_computation.2 | async-start | bytes 4423680 | tf_op jit(solution)/shard_map/all_gather | solution.py:85
  8.7 15.3 %collective-permute-start.3 = (bf16[64,27,64]{0,2,1:T(8,128)(2,1)S(1)}, bf16[64,27,64]{0,2,1:T(8,128)(2,1)S(1)}, u32[]{:S(2)}, u32[]{:S(2)}) collective-permute-start(bf16[64,27,64]{0,2,1:T(8,128)(2,1)S(1)} %bitcast.85), channel_id=1, source_target_pairs={{0,4},{4,8},{8,12},{12,0},{1,5},{5,9},{9,13},{13,1},{2,6},{6,10},{... | collective-permute-start | bytes 663560 | tf_op jit(solution)/shard_map/ppermute | solution.py:78
  24.0 13.1 %collective-permute-start.4 = (bf16[64,27,64]{0,2,1:T(8,128)(2,1)S(1)}, bf16[64,27,64]{0,2,1:T(8,128)(2,1)S(1)}, u32[]{:S(2)}, u32[]{:S(2)}) collective-permute-start(bf16[64,27,64]{0,2,1:T(8,128)(2,1)S(1)} %collective-permute-done.3), channel_id=1, source_target_pairs={{0,4},{4,8},{8,12},{12,0},{1,5},{5,9},{9,13},{13,1},{2,6},{6,10},{... | collective-permute-start | bytes 663560 | tf_op jit(solution)/shard_map/ppermute | solution.py:78
  37.2 12.3 %collective-permute-start.5 = (bf16[64,27,64]{0,2,1:T(8,128)(2,1)S(1)}, bf16[64,27,64]{0,2,1:T(8,128)(2,1)S(1)}, u32[]{:S(2)}, u32[]{:S(2)}) collective-permute-start(bf16[64,27,64]{0,2,1:T(8,128)(2,1)S(1)} %collective-permute-done.4), channel_id=1, source_target_pairs={{0,4},{4,8},{8,12},{12,0},{1,5},{5,9},{9,13},{13,1},{2,6},{6,10},{... | collective-permute-start | bytes 663560 | tf_op jit(solution)/shard_map/ppermute | solution.py:78
  54.7 11.8 %copy-start.1 = (bf16[1,4,4,16,256]{4,3,2,1,0:T(8,128)(2,1)S(1)}, bf16[1,4,4,16,256]{4,3,2,1,0:T(8,128)(2,1)}, u32[]{:S(2)}) copy-start(bf16[1,4,4,16,256]{4,3,2,1,0:T(8,128)(2,1)} %param.11) | copy-start | bytes 393220
  54.7 76.5 %all-gather.5.cloned.1.call-start = ((), (), s32[]{:S(2)}) async-start(), calls=%async_computation.3 | async-start | bytes 4423680 | tf_op jit(solution)/shard_map/all_gather | solution.py:85
  55.0 11.5 %collective-permute-start.9 = (bf16[64,27,64]{0,2,1:T(8,128)(2,1)S(1)}, bf16[64,27,64]{0,2,1:T(8,128)(2,1)S(1)}, u32[]{:S(2)}, u32[]{:S(2)}) collective-permute-start(bf16[64,27,64]{0,2,1:T(8,128)(2,1)S(1)} %bitcast.87), channel_id=1, source_target_pairs={{0,4},{4,8},{8,12},{12,0},{1,5},{5,9},{9,13},{13,1},{2,6},{6,10},{... | collective-permute-start | bytes 663560 | tf_op jit(solution)/shard_map/ppermute | solution.py:78
  66.5 10.6 %collective-permute-start.10 = (bf16[64,27,64]{0,2,1:T(8,128)(2,1)S(1)}, bf16[64,27,64]{0,2,1:T(8,128)(2,1)S(1)}, u32[]{:S(2)}, u32[]{:S(2)}) collective-permute-start(bf16[64,27,64]{0,2,1:T(8,128)(2,1)S(1)} %collective-permute-done.9), channel_id=1, source_target_pairs={{0,4},{4,8},{8,12},{12,0},{1,5},{5,9},{9,13},{13,1},{2,6},{6,10},{... | collective-permute-start | bytes 663560 | tf_op jit(solution)/shard_map/ppermute | solution.py:78
  77.0 10.1 %collective-permute-start.11 = (bf16[64,27,64]{0,2,1:T(8,128)(2,1)S(1)}, bf16[64,27,64]{0,2,1:T(8,128)(2,1)S(1)}, u32[]{:S(2)}, u32[]{:S(2)}) collective-permute-start(bf16[64,27,64]{0,2,1:T(8,128)(2,1)S(1)} %collective-permute-done.10), channel_id=1, source_target_pairs={{0,4},{4,8},{8,12},{12,0},{1,5},{5,9},{9,13},{13,1},{2,6},{6,10},{... | collective-permute-start | bytes 663560 | tf_op jit(solution)/shard_map/ppermute | solution.py:78
  77.0 15.4 %copy-start.4 = (f32[3,256]{1,0:T(4,128)S(1)}, f32[3,256]{1,0:T(4,128)}, u32[]{:S(2)}) copy-start(f32[3,256]{1,0:T(4,128)} %param.14) | copy-start | bytes 9220
  92.4 1.5 copy-start.5
  92.4 1.5 copy-start.6
  92.6 3.2 %collective-permute-start = (bf16[2,4,16,256]{3,2,1,0:T(8,128)(2,1)S(1)}, bf16[2,4,16,256]{3,2,1,0:T(8,128)(2,1)S(1)}, u32[]{:S(2)}, u32[]{:S(2)}) collective-permute-start(bf16[2,4,16,256]{3,2,1,0:T(8,128)(2,1)S(1)} %slice.322), channel_id=1, source_target_pairs={{0,4},{4,8},{8,12},{1,5},{5,9},{9,13},{2,6},{6,10},{10,14},{3,7},{... | collective-permute-start | bytes 196616 | tf_op jit(solution)/shard_map/ppermute | solution.py:10
  95.8 5.2 %collective-permute-start.1 = (bf16[6,1,16,256]{3,2,1,0:T(8,128)(2,1)S(1)}, bf16[6,1,16,256]{3,2,1,0:T(8,128)(2,1)S(1)}, u32[]{:S(2)}, u32[]{:S(2)}) collective-permute-start(bf16[6,1,16,256]{3,2,1,0:T(8,128)(2,1)S(1)} %get-tuple-element.72), channel_id=1, source_target_pairs={{0,2},{1,3},{4,6},{5,7},{8,10},{9,11},{12,14},{13,15},{16,18},{17,... | collective-permute-start | bytes 147464 | tf_op jit(solution)/shard_map/ppermute | solution.py:21
  98.4 7.2 %collective-permute-start.2 = (bf16[6,1,16,256]{3,2,1,0:T(8,128)(2,1)S(1)}, bf16[6,1,16,256]{3,2,1,0:T(8,128)(2,1)S(1)}, u32[]{:S(2)}, u32[]{:S(2)}) collective-permute-start(bf16[6,1,16,256]{3,2,1,0:T(8,128)(2,1)S(1)} %get-tuple-element.73), channel_id=1, source_target_pairs={{2,0},{3,1},{6,4},{7,5},{10,8},{11,9},{14,12},{15,13},{18,16},{19,... | collective-permute-start | bytes 147464 | tf_op jit(solution)/shard_map/ppermute | solution.py:23
  117.6 8.4 %collective-permute-start.6 = (bf16[2,4,16,256]{3,2,1,0:T(8,128)(2,1)S(1)}, bf16[2,4,16,256]{3,2,1,0:T(8,128)(2,1)S(1)}, u32[]{:S(2)}, u32[]{:S(2)}) collective-permute-start(bf16[2,4,16,256]{3,2,1,0:T(8,128)(2,1)S(1)} %slice.356), channel_id=1, source_target_pairs={{0,4},{4,8},{8,12},{1,5},{5,9},{9,13},{2,6},{6,10},{10,14},{3,7},{... | collective-permute-start | bytes 196616 | tf_op jit(solution)/shard_map/ppermute | solution.py:10
  122.7 17.3 %all-to-all-start.1 = ((bf16[8,1,9]{2,1,0:T(2,128)(2,1)}), bf16[8,1,9]{2,1,0:T(2,128)(2,1)S(1)}, u32[]{:S(2)}, u32[]{:S(2)}) async-start(bf16[8,1,9]{2,1,0:T(2,128)(2,1)} %all_to_all.12), calls=%async_computation.1 | async-start | bytes 8192 | tf_op jit(solution)/shard_map/all_to_all | solution.py:133
  126.0 7.4 %collective-permute-start.7 = (bf16[6,1,16,256]{3,2,1,0:T(8,128)(2,1)S(1)}, bf16[6,1,16,256]{3,2,1,0:T(8,128)(2,1)S(1)}, u32[]{:S(2)}, u32[]{:S(2)}) collective-permute-start(bf16[6,1,16,256]{3,2,1,0:T(8,128)(2,1)S(1)} %get-tuple-element.66), channel_id=1, source_target_pairs={{0,2},{1,3},{4,6},{5,7},{8,10},{9,11},{12,14},{13,15},{16,18},{17,... | collective-permute-start | bytes 147464 | tf_op jit(solution)/shard_map/ppermute | solution.py:21
  129.9 6.0 %collective-permute-start.8 = (bf16[6,1,16,256]{3,2,1,0:T(8,128)(2,1)S(1)}, bf16[6,1,16,256]{3,2,1,0:T(8,128)(2,1)S(1)}, u32[]{:S(2)}, u32[]{:S(2)}) collective-permute-start(bf16[6,1,16,256]{3,2,1,0:T(8,128)(2,1)S(1)} %get-tuple-element.67), channel_id=1, source_target_pairs={{2,0},{3,1},{6,4},{7,5},{10,8},{11,9},{14,12},{15,13},{18,16},{19,... | collective-permute-start | bytes 147464 | tf_op jit(solution)/shard_map/ppermute | solution.py:23
  138.0 0.7 copy-start.3
  138.0 13.3 %copy-start.2 = (f32[3072]{0:T(1024)S(1)}, f32[3072]{0:T(1024)}, u32[]{:S(2)}) copy-start(f32[3072]{0:T(1024)} %param.19) | copy-start | bytes 36868
  140.1 11.1 %all-to-all-start = ((bf16[8,2,288]{2,1,0:T(2,128)(2,1)}), bf16[8,2,288]{2,1,0:T(2,128)(2,1)S(1)}, u32[]{:S(2)}, u32[]{:S(2)}) async-start(bf16[8,2,288]{2,1,0:T(2,128)(2,1)} %reshape.166), calls=%async_computation | async-start | bytes 24576 | tf_op jit(solution)/shard_map/all_to_all | solution.py:132
Sparse Core Ops, SparseCore 0:
  54.8 28.4 all-gather.2
  92.6 28.5 all-gather.4
